TPU v7x, 128 devices: a whole 4x4x4 slice. The times are simulated.
128 devices in a mesh: grp: 2 (over x_lo), tile: 64 (over z, y, x_hi, core).
Axes of the slice: x: 4 (x_hi: 2, x_lo: 2; x = x_hi * 2 + x_lo), y: 4, z: 4, core: 2. Of those that a mesh axis runs over, the one named last changes fastest.
Arguments:
- ocean_state: float32 [3, 24, 1024, 4096], P(None, None, 'tile', 'grp'), may hold values from -6 to 6
- biharmonic: float32 [1024, 4096], P('tile', 'grp'), may hold values from 0.004 to 0.014
- prev_stress: float32 [2, 1024, 4096], P(None, 'tile', 'grp'), may hold values from -4 to 4
- ice_state: float32 [5, 1024, 4096], P(None, 'tile', 'grp'), may hold values from -2 to 2
- strength: float32 [1024, 4096], P('tile', 'grp'), may hold values from 0.5 to 2
- ice_mass: float32 [1024, 4096], P('tile', 'grp'), may hold values from 0.5 to 2
- ice_fraction: float32 [1024, 4096], P('tile', 'grp'), may hold values from 0.15 to 1
- wind_stress: float32 [2, 1024, 4096], P(None, 'tile', 'grp'), may hold values from -2 to 2
- ice_count: int32 [128], P(('grp', 'tile')), may hold values from 0 to 16, as said below
- ice_list: int32 [128, 16], P(('grp', 'tile')), may hold values from 0 to 15, as said below
Outputs:
- ocean_out: float32 [3, 24, 1024, 4096], P(None, None, 'tile', 'grp')
- ice_out: float32 [5, 1024, 4096], P(None, 'tile', 'grp')
- stress_out: float32 [2, 1024, 4096], P(None, 'tile', 'grp')
Inputs may be any that keep to these rules, and one draw needn't show every extreme that they name: `ice_count`: the tiles g * 64 + t and g * 64 + (t + 64 / 2) % 64 together have at most 16 ice-covered blocks, and some such pair has exactly 16; tiles near the first and last rows have the most. `ice_list`: each row is an ordering of the tile's 16 block numbers.
All inputs are finite; a program needn't handle non-finite values.
Results may differ from a plain program's by a relative error of at most 0.00002.
Values sent between devices are 32-bit elements; how exact they have to be, the bound alone decides.
A program may use at most 192 MiB of HBM per device.

v0:
```python
import jax
import jax.numpy as jnp
from jax import lax
from jax.sharding import PartitionSpec as P

BY = 16
BX = 128
SUBCYCLES = 64


kv_mix = 0.2
relax_rate = 0.5
sub_step = 0.3
drag_coef = 1.0
turning = 0.3
delta_min = 0.5
coriolis_scale = 0.2


def padded_2(x, sides, width, wrap):
    for axis, dim in sides:
        size, length = (lax.axis_size(axis), x.shape[dim])
        up = [(i, (i + 1) % size) for i in range(size if wrap else size - 1)]
        down = [(j, i) for i, j in up]
        last = lax.slice_in_dim(x, length - width, length, axis=dim)
        leading = lax.slice_in_dim(x, 0, width, axis=dim)
        before = lax.ppermute(last, axis, up)
        after = lax.ppermute(leading, axis, down)
        x = jnp.concatenate([before, x, after], axis=dim)
    return x


def ahead_diff(field, axis):
    length = field.shape[axis]
    inner = lax.slice_in_dim(field, 1, length, axis=axis) - lax.slice_in_dim(
        field, 0, length - 1, axis=axis
    )
    return jnp.concatenate(
        [inner, jnp.zeros_like(lax.slice_in_dim(field, 0, 1, axis=axis))], axis=axis
    )


def behind_diff(field, axis):
    length = field.shape[axis]
    inner = lax.slice_in_dim(field, 1, length, axis=axis) - lax.slice_in_dim(
        field, 0, length - 1, axis=axis
    )
    return jnp.concatenate([lax.slice_in_dim(field, 0, 1, axis=axis), inner], axis=axis)


def ice_dynamics(fields, y_axis, x_axis):
    (
        vel_x,
        vel_y,
        stress_xx,
        stress_yy,
        stress_xy,
        ice_strength,
        mass,
        fraction,
        wind_x,
        wind_y,
        ocean_x,
        ocean_y,
    ) = fields
    pressure = relax_rate * ice_strength
    inertia = mass + sub_step * drag_coef

    def subcycle(step_index, carry):
        vel_x, vel_y, stress_xx, stress_yy, stress_xy = carry
        du_dx = ahead_diff(vel_x, x_axis)
        du_dy = ahead_diff(vel_x, y_axis)
        dv_dx = ahead_diff(vel_y, x_axis)
        dv_dy = ahead_diff(vel_y, y_axis)
        divergence = du_dx + dv_dy
        tension = du_dx - dv_dy
        shearing = du_dy + dv_dx
        deform = jnp.sqrt(
            divergence * divergence
            + 0.25 * (tension * tension + shearing * shearing)
            + delta_min * delta_min
        )
        sigma_one = (stress_xx + stress_yy + pressure * (divergence / deform - 1.0)) / (
            1.0 + relax_rate
        )
        sigma_two = (stress_xx - stress_yy + 0.25 * pressure * tension / deform) / (
            1.0 + relax_rate
        )
        stress_xy = (stress_xy + 0.125 * pressure * shearing / deform) / (1.0 + relax_rate)
        stress_xx = 0.5 * (sigma_one + sigma_two)
        stress_yy = 0.5 * (sigma_one - sigma_two)
        force_x = behind_diff(stress_xx, x_axis) + behind_diff(stress_xy, y_axis)
        force_y = behind_diff(stress_xy, x_axis) + behind_diff(stress_yy, y_axis)
        new_x = (
            mass * vel_x
            + sub_step * (force_x + wind_x + drag_coef * ocean_x + turning * mass * vel_y)
        ) / inertia
        new_y = (
            mass * vel_y
            + sub_step * (force_y + wind_y + drag_coef * ocean_y - turning * mass * vel_x)
        ) / inertia
        return (new_x, new_y, stress_xx, stress_yy, stress_xy)

    vel_x, vel_y, stress_xx, stress_yy, stress_xy = lax.fori_loop(
        0, SUBCYCLES, subcycle, (vel_x, vel_y, stress_xx, stress_yy, stress_xy)
    )
    drag_x = fraction * drag_coef * (vel_x - ocean_x) + (1.0 - fraction) * wind_x
    drag_y = fraction * drag_coef * (vel_y - ocean_y) + (1.0 - fraction) * wind_y
    return (vel_x, vel_y, stress_xx, stress_yy, stress_xy, drag_x, drag_y)


def run_blocks(blocks):
    return jnp.stack(ice_dynamics([blocks[:, index] for index in range(12)], 1, 2), axis=1)


def laplace(padded):
    return (
        padded[..., 1:-1, 2:]
        + padded[..., 1:-1, :-2]
        + padded[..., 2:, 1:-1]
        + padded[..., :-2, 1:-1]
        - 4.0 * padded[..., 1:-1, 1:-1]
    )


def vertical(field):
    upper = jnp.concatenate([field[:1], field[:-1]], axis=0)
    lower = jnp.concatenate([field[1:], field[-1:]], axis=0)
    return upper + lower - 2.0 * field


def ocean_field(padded, field, biharmonic):
    return field - biharmonic * laplace(laplace(padded)) + kv_mix * vertical(field)


def per_device(
    ocean_state,
    biharmonic,
    prev_stress,
    ice_state,
    strength,
    ice_mass,
    ice_fraction,
    wind_stress,
    ice_count,
    ice_list,
):
    tile_rows = ocean_state.shape[2]
    tile_cols = ocean_state.shape[3]
    total_rows = tile_rows * lax.axis_size("tile")
    row_padded = padded_2(ocean_state, (("tile", 2),), 2, False)
    padded = padded_2(row_padded, (("grp", 3),), 2, True)
    rows = (lax.axis_index("tile") * tile_rows + jnp.arange(tile_rows)).astype(jnp.float32) + 0.5
    coriolis = (coriolis_scale * (2.0 * rows / total_rows - 1.0))[:, None]
    mixed = [ocean_field(padded[index], ocean_state[index], biharmonic) for index in range(3)]
    east = mixed[0] + coriolis * ocean_state[1]
    north = mixed[1] - coriolis * ocean_state[0]
    east = east.at[0].add(prev_stress[0])
    north = north.at[0].add(prev_stress[1])
    ocean_out = jnp.stack([east, north, mixed[2]])
    row_blocks = tile_rows // BY
    col_blocks = tile_cols // BX
    block_total = row_blocks * col_blocks
    stacked = jnp.stack(
        [
            ice_state[0],
            ice_state[1],
            ice_state[2],
            ice_state[3],
            ice_state[4],
            strength,
            ice_mass,
            ice_fraction,
            wind_stress[0],
            wind_stress[1],
            ocean_state[0, 0],
            ocean_state[1, 0],
        ]
    )
    blocks = (
        stacked.reshape(12, row_blocks, BY, col_blocks, BX)
        .transpose(1, 3, 0, 2, 4)
        .reshape(block_total, 12, BY, BX)
    )
    count = ice_count[0]
    listed_blocks = ice_list[0]
    slots = jnp.arange(block_total, dtype=jnp.int32)
    position = jnp.sum(
        jnp.where(listed_blocks[:, None] == slots[None, :], slots[:, None], 0), axis=0
    )
    covered = position < count
    results = run_blocks(blocks)
    mask = covered[:, None, None, None]
    new_state = jnp.where(mask, results[:, :5], blocks[:, :5])
    new_stress = jnp.where(mask, results[:, 5:7], blocks[:, 8:10])
    combined = jnp.concatenate([new_state, new_stress], axis=1)
    combined = (
        combined.reshape(row_blocks, col_blocks, 7, BY, BX)
        .transpose(2, 0, 3, 1, 4)
        .reshape(7, tile_rows, tile_cols)
    )
    return (ocean_out, combined[:5], combined[5:])


def solution(mesh):
    placed = (
        P(None, None, "tile", "grp"),
        P("tile", "grp"),
        P(None, "tile", "grp"),
        P(None, "tile", "grp"),
        P("tile", "grp"),
        P("tile", "grp"),
        P("tile", "grp"),
        P(None, "tile", "grp"),
        P(("grp", "tile")),
        P(("grp", "tile"), None),
    )
    return jax.shard_map(
        per_device,
        mesh=mesh,
        in_specs=placed,
        out_specs=(P(None, None, "tile", "grp"), P(None, "tile", "grp"), P(None, "tile", "grp")),
        check_vma=False,
    )
```

profile of v0, /device:TPU:96, one launch (start us, length us, event | category | flops | bytes accessed | tf_op | source)
XLA Modules:
  0.0 221.2 jit_solution(5527433677608715708)
XLA Ops:
  0.6 6.5 %fusion.42 = (f32[3,24,2,2048]{3,2,1,0:T(2,128)}, f32[3,24,2,2048]{3,2,1,0:T(2,128)}) fusion(f32[3,24,16,2048]{3,2,1,0:T(8,128)} %param.16), kind=kLoop, calls=%fused_computation.148 | loop fusion | bytes 4718592 | tf_op jit(solution)/shard_map/slice | solution.py:25
  7.1 6.8 %collective-permute-start.1 = (f32[3,24,2,2048]{3,2,1,0:T(2,128)}, f32[3,24,2,2048]{3,2,1,0:T(2,128)}, u32[]{:S(2)}, u32[]{:S(2)}) collective-permute-start(f32[3,24,2,2048]{3,2,1,0:T(2,128)} %get-tuple-element.308), channel_id=1, source_target_pairs={{1,0},{2,1},{3,2},{4,3},{5,4},{6,5},{7,6},{8,7},{9,8},{10,9},{11,1... | collective-permute-start | bytes 3538952 | tf_op jit(solution)/shard_map/ppermute | solution.py:28
  13.9 1.9 collective-permute-start
  15.9 2.0 slice_bitcast_fusion.24
  19.3 58.3 %while.22 = (s32[]{:T(128)}, f32[16,16,128]{2,1,0:T(8,128)S(1)}, f32[16,16,128]{2,1,0:T(8,128)S(1)}, f32[16,16,128]{2,1,0:T(8,128)S(1)}, f32[16,16,128]{2,1,0:T(...) while((s32[]{:T(128)}, f32[16,16,128]{2,1,0:T(8,128)S(1)}, ...), condition=%wide.region_2.3_spmd, body=%wide.region_1.0_spmd.sunk | while | flops 2022402 | bytes 6850693 | solution.py:104
  20.0 0.2 fusion.44
  20.9 0.2 fusion.44
  21.8 0.2 fusion.44
  22.7 0.2 fusion.44
  23.6 0.2 fusion.44
  24.6 0.2 fusion.44
  25.5 0.2 fusion.44
  26.4 0.2 fusion.44
  27.3 0.2 fusion.44
  28.2 0.2 fusion.44
  29.1 0.2 fusion.44
  30.0 0.2 fusion.44
  30.9 0.2 fusion.44
  31.8 0.2 fusion.44
  32.8 0.2 fusion.44
  33.7 0.2 fusion.44
  34.6 0.2 fusion.44
  35.5 0.2 fusion.44
  36.4 0.2 fusion.44
  37.3 0.2 fusion.44
  38.2 0.2 fusion.44
  39.1 0.2 fusion.44
  40.0 0.2 fusion.44
  41.0 0.2 fusion.44
  41.9 0.2 fusion.44
  42.8 0.2 fusion.44
  43.7 0.2 fusion.44
  44.6 0.2 fusion.44
  45.5 0.2 fusion.44
  46.4 0.2 fusion.44
  47.3 0.2 fusion.44
  48.2 0.2 fusion.44
  49.2 0.2 fusion.44
  79.1 14.1 %slice_bitcast_fusion.7 = (f32[23,16,2048]{2,1,0:T(8,128)}, f32[23,16,2048]{2,1,0:T(8,128)}, f32[23,16,2048]{2,1,0:T(8,128)}, f32[23,16,2048]{2,1,0:T(8,128)}, f...) fusion(f32[3,24,16,2048]{3,2,1,0:T(8,128)} %param.16), kind=kLoop, calls=%fused_computation.96 | loop fusion | bytes 36175872 | tf_op jit(solution)/shard_map/slice | solution.py:128
  93.4 0.8 slice-done.2
  94.2 3.9 %pad_maximum_fusion = f32[3,24,20,2048]{3,2,1,0:T(8,128)S(1)} fusion(f32[3,24,2,2048]{3,2,1,0:T(2,128)} %collective-permute-done.1, f32[3,24,16,2048]{3,2,1,0:T(8,128)S(1)} %bitcast.181, f32[3,24,2,2048]{3,2,1,0:T(2,128)} %collective-permute-done), kind=kLoop, calls=%fused_computation.31 | loop fusion | flops 5898240 | bytes 23592960 | tf_op jit(solution)/shard_map/concatenate | solution.py:29
  98.1 5.0 %copy-done = f32[3,24,20,2048]{3,2,1,0:T(8,128)} copy-done((f32[3,24,20,2048]{3,2,1,0:T(8,128)}, f32[3,24,20,2048]{3,2,1,0:T(8,128)S(1)}, u32[]{:S(2)}) %copy-start) | copy-done | bytes 11796504
  103.1 0.3 fusion.41
  103.4 0.4 copy.102
  103.9 0.6 collective-permute-start.2
  104.5 0.4 copy.103
  105.0 1.7 collective-permute-start.3
  106.8 0.9 slice.528
  107.7 0.7 slice.530
  108.4 0.5 copy.104
  108.9 0.5 collective-permute-done.3
  109.4 0.5 copy.105
  109.9 18.3 %concatenate.71 = f32[3,24,20,2052]{3,2,1,0:T(8,128)} concatenate(f32[3,24,20,2]{3,2,1,0:T(8,128)S(1)} %copy.104, f32[3,24,20,2048]{3,2,1,0:T(8,128)} %copy-done, f32[3,24,20,2]{3,2,1,0:T(8,128)S(1)} %copy.105), dimensions={3} | concatenate | bytes 23639040 | tf_op jit(solution)/shard_map/concatenate | solution.py:29
  128.2 11.1 %slice_bitcast_fusion.2 = (f32[24,20,2052]{2,1,0:T(8,128)}, f32[24,20,2052]{2,1,0:T(8,128)}, f32[24,20,2052]{2,1,0:T(8,128)}) fusion(f32[3,24,20,2052]{3,2,1,0:T(8,128)} %concatenate.71), kind=kLoop, calls=%fused_computation.50 | loop fusion | bytes 23639040 | tf_op jit(solution)/shard_map/squeeze | solution.py:155
  139.3 15.5 %fusion.14 = f32[24,18,2050]{2,1,0:T(8,128)S(1)} fusion(f32[24,20,2052]{2,1,0:T(8,128)} %get-tuple-element.288), kind=kLoop, calls=%fused_computation.46 | loop fusion | flops 4428000 | bytes 21254400 | tf_op jit(solution)/shard_map/sub | solution.py:118
  154.9 6.8 %fusion.29 = f32[24,16,2048]{2,1,0:T(8,128)} fusion(f32[24,18,2050]{2,1,0:T(8,128)S(1)} %fusion.14, f32[23,16,2048]{2,1,0:T(8,128)} %get-tuple-element.305, f32[1,16,2048]{2,1,0:T(8,128)S(1)} %copy-done.4, f32[1,16,2048]{2,1,0:T(8,128)S(1)} %copy-done.3, f32[23,16,2048]{2,1,0:T(8,128)} %get-tuple-element.301, f32[3,24,16,2048]{3,2,1,0:T(8,128)S(1)} %bitcast.183, ...), kind=kLoop, calls=%fused_computation.74 | loop fusion | flops 12582912 | bytes 31588416 | tf_op jit(solution)/shard_map/add | solution.py:156
  161.7 1.9 copy.144
  163.6 31.4 %fusion.12 = (f32[24,18,2050]{2,1,0:T(8,128)}, f32[24,18,2050]{2,1,0:T(8,128)}) fusion(f32[24,20,2052]{2,1,0:T(8,128)} %get-tuple-element.289, f32[24,20,2052]{2,1,0:T(8,128)} %get-tuple-element.290), kind=kLoop, calls=%fused_computation.34 | loop fusion | flops 8856000 | bytes 42508800 | tf_op jit(solution)/shard_map/sub | solution.py:118
  195.1 13.7 %fusion.24 = f32[24,16,2048]{2,1,0:T(8,128)S(1)} fusion(f32[24,18,2050]{2,1,0:T(8,128)} %get-tuple-element.325, f32[23,16,2048]{2,1,0:T(8,128)} %get-tuple-element.304, f32[1,16,2048]{2,1,0:T(8,128)} %get-tuple-element.297, f32[1,16,2048]{2,1,0:T(8,128)} %get-tuple-element.296, f32[23,16,2048]{2,1,0:T(8,128)} %get-tuple-element.303, ...), kind=kLoop, calls=%fused_computation.65 | loop fusion | flops 12582912 | bytes 31588416 | tf_op jit(solution)/shard_map/sub | solution.py:157
  208.8 0.3 copy.145
  209.1 0.6 copy-done.5
  209.7 0.9 fusion.40
  210.7 5.9 %fusion.19 = f32[1,24,16,2048]{3,2,1,0:T(8,128)S(1)} fusion(f32[24,18,2050]{2,1,0:T(8,128)S(1)} %bitcast.186, f32[23,16,2048]{2,1,0:T(8,128)} %get-tuple-element.302, f32[1,16,2048]{2,1,0:T(8,128)S(1)} %get-tuple-element.295, f32[1,16,2048]{2,1,0:T(8,128)S(1)} %get-tuple-element.300, f32[23,16,2048]{2,1,0:T(8,128)} %get-tuple-element.306, ...), kind=kLoop, calls=%fused_computation.56 | loop fusion | flops 11010048 | bytes 28442624 | tf_op jit(solution)/shard_map/stack | solution.py:160
  216.6 4.6 %pad_maximum_fusion.1 = f32[3,24,16,2048]{3,2,1,0:T(8,128)} fusion(f32[1,24,16,2048]{3,2,1,0:T(8,128)S(1)} %fusion.19, f32[1,24,16,2048]{3,2,1,0:T(8,128)S(1)} %get-tuple-element.323, f32[1,24,16,2048]{3,2,1,0:T(8,128)S(1)} %get-tuple-element.322), kind=kLoop, calls=%fused_computation.32 | loop fusion | flops 4718592 | bytes 18874368 | tf_op jit(solution)/shard_map/stack | solution.py:160
  (754 shorter events, 48.1 us)
Async XLA Ops:
  0.6 17.3 %copy-start.2 = (f32[5,16,2048]{2,1,0:T(8,128)S(1)}, f32[5,16,2048]{2,1,0:T(8,128)}, u32[]{:S(2)}) copy-start(f32[5,16,2048]{2,1,0:T(8,128)} %param.19) | copy-start | bytes 1966084
  7.1 11.0 %copy-start.7 = (f32[16,2048]{1,0:T(8,128)S(1)}, f32[16,2048]{1,0:T(8,128)}, u32[]{:S(2)}) copy-start(f32[16,2048]{1,0:T(8,128)} %param.20) | copy-start | bytes 393220
  7.1 11.0 %copy-start.8 = (f32[16,2048]{1,0:T(8,128)S(1)}, f32[16,2048]{1,0:T(8,128)}, u32[]{:S(2)}) copy-start(f32[16,2048]{1,0:T(8,128)} %param.21) | copy-start | bytes 393220
  7.1 11.1 %copy-start.9 = (f32[16,2048]{1,0:T(8,128)S(1)}, f32[16,2048]{1,0:T(8,128)}, u32[]{:S(2)}) copy-start(f32[16,2048]{1,0:T(8,128)} %param.22) | copy-start | bytes 393220
  7.1 11.1 %copy-start.6 = (f32[2,16,2048]{2,1,0:T(8,128)S(1)}, f32[2,16,2048]{2,1,0:T(8,128)}, u32[]{:S(2)}) copy-start(f32[2,16,2048]{2,1,0:T(8,128)} %param.23) | copy-start | bytes 786436
  7.1 86.1 %collective-permute-start.1 = (f32[3,24,2,2048]{3,2,1,0:T(2,128)}, f32[3,24,2,2048]{3,2,1,0:T(2,128)}, u32[]{:S(2)}, u32[]{:S(2)}) collective-permute-start(f32[3,24,2,2048]{3,2,1,0:T(2,128)} %get-tuple-element.308), channel_id=1, source_target_pairs={{1,0},{2,1},{3,2},{4,3},{5,4},{6,5},{7,6},{8,7},{9,8},{10,9},{11,1... | collective-permute-start | bytes 3538952 | tf_op jit(solution)/shard_map/ppermute | solution.py:28
  13.9 79.3 %collective-permute-start = (f32[3,24,2,2048]{3,2,1,0:T(2,128)}, f32[3,24,2,2048]{3,2,1,0:T(2,128)}, u32[]{:S(2)}, u32[]{:S(2)}) collective-permute-start(f32[3,24,2,2048]{3,2,1,0:T(2,128)} %get-tuple-element.307), channel_id=1, source_target_pairs={{0,1},{1,2},{2,3},{3,4},{4,5},{5,6},{6,7},{7,8},{8,9},{9,10},{10,1... | collective-permute-start | bytes 3538952 | tf_op jit(solution)/shard_map/ppermute | solution.py:27
  19.3 58.5 %copy-start.10 = (s32[1,16]{1,0:T(1,128)S(1)}, s32[1,16]{1,0:T(1,128)}, u32[]{:S(2)}) copy-start(s32[1,16]{1,0:T(1,128)} %param.25) | copy-start | bytes 196
  79.0 14.2 %slice-start = ((s8[9437184]{0:T(1024)(128)(4,1)}), s8[4194304]{0:T(1024)(128)(4,1)S(1)}, s32[]{:S(2)}) async-start(s8[9437184]{0:T(1024)(128)(4,1)} %bitcast.180), calls=%async_computation | async-start | bytes 8388608
  79.1 14.3 %slice-start.1 = ((s8[9437184]{0:T(1024)(128)(4,1)}), s8[4194304]{0:T(1024)(128)(4,1)S(1)}, s32[]{:S(2)}) async-start(s8[9437184]{0:T(1024)(128)(4,1)} %bitcast.180), calls=%async_computation.1 | async-start | bytes 8388608
  79.1 15.1 %slice-start.2 = ((s8[9437184]{0:T(1024)(128)(4,1)}), s8[1048576]{0:T(1024)(128)(4,1)S(1)}, s32[]{:S(2)}) async-start(s8[9437184]{0:T(1024)(128)(4,1)} %bitcast.180), calls=%async_computation.2 | async-start | bytes 2097152
  98.1 5.0 %copy-start = (f32[3,24,20,2048]{3,2,1,0:T(8,128)}, f32[3,24,20,2048]{3,2,1,0:T(8,128)S(1)}, u32[]{:S(2)}) copy-start(f32[3,24,20,2048]{3,2,1,0:T(8,128)S(1)} %pad_maximum_fusion) | copy-start | bytes 35389444
  103.9 4.6 %collective-permute-start.2 = (f32[3,24,20,2]{1,3,2,0:T(2,128)S(1)}, f32[3,24,20,2]{1,3,2,0:T(2,128)S(1)}, u32[]{:S(2)}, u32[]{:S(2)}) collective-permute-start(f32[3,24,20,2]{1,3,2,0:T(2,128)S(1)} %copy.102), channel_id=1, source_target_pairs={{0,64},{64,0},{1,65},{65,1},{2,66},{66,2},{3,67},{67,3},{4,68},{68... | collective-permute-start | bytes 34568 | tf_op jit(solution)/shard_map/ppermute | solution.py:27
  105.0 4.5 %collective-permute-start.3 = (f32[3,24,20,2]{1,3,2,0:T(2,128)S(1)}, f32[3,24,20,2]{1,3,2,0:T(2,128)S(1)}, u32[]{:S(2)}, u32[]{:S(2)}) collective-permute-start(f32[3,24,20,2]{1,3,2,0:T(2,128)S(1)} %copy.103), channel_id=1, source_target_pairs={{64,0},{0,64},{65,1},{1,65},{66,2},{2,66},{67,3},{3,67},{68,4},{4,... | collective-permute-start | bytes 34568 | tf_op jit(solution)/shard_map/ppermute | solution.py:28
  139.3 15.5 %slice-start.3 = ((s8[9437184]{0:T(1024)(128)(4,1)}), s8[4194304]{0:T(1024)(128)(4,1)S(1)}, s32[]{:S(2)}) async-start(s8[9437184]{0:T(1024)(128)(4,1)} %bitcast.182), calls=%async_computation.3 | async-start | bytes 8388608
  139.3 15.5 %slice-start.4 = ((s8[9437184]{0:T(1024)(128)(4,1)}), s8[4194304]{0:T(1024)(128)(4,1)S(1)}, s32[]{:S(2)}) async-start(s8[9437184]{0:T(1024)(128)(4,1)} %bitcast.182), calls=%async_computation.4 | async-start | bytes 8388608
  139.3 15.5 %slice-start.5 = ((s8[9437184]{0:T(1024)(128)(4,1)}), s8[1048576]{0:T(1024)(128)(4,1)S(1)}, s32[]{:S(2)}) async-start(s8[9437184]{0:T(1024)(128)(4,1)} %bitcast.182), calls=%async_computation.5 | async-start | bytes 2097152
  139.3 15.6 %copy-start.1 = (f32[16,2048]{1,0:T(8,128)S(1)}, f32[16,2048]{1,0:T(8,128)}, u32[]{:S(2)}) copy-start(f32[16,2048]{1,0:T(8,128)} %param.17) | copy-start | bytes 393220
  139.3 15.6 %copy-start.3 = (f32[1,16,2048]{2,1,0:T(8,128)S(1)}, f32[1,16,2048]{2,1,0:T(8,128)}, u32[]{:S(2)}) copy-start(f32[1,16,2048]{2,1,0:T(8,128)} %get-tuple-element.298) | copy-start | bytes 393220
  139.3 15.6 %copy-start.4 = (f32[1,16,2048]{2,1,0:T(8,128)S(1)}, f32[1,16,2048]{2,1,0:T(8,128)}, u32[]{:S(2)}) copy-start(f32[1,16,2048]{2,1,0:T(8,128)} %get-tuple-element.299) | copy-start | bytes 393220
  195.0 15.6 %slice-start.6 = ((s8[5013504]{0:T(1024)(128)(4,1)}), s8[4194304]{0:T(1024)(128)(4,1)S(1)}, s32[]{:S(2)}) async-start(s8[5013504]{0:T(1024)(128)(4,1)} %bitcast.185), calls=%async_computation.6 | async-start | bytes 8388608
  195.0 15.6 %slice-start.7 = ((s8[5013504]{0:T(1024)(128)(4,1)}), s8[819200]{0:T(1024)(128)(4,1)S(1)}, s32[]{:S(2)}) async-start(s8[5013504]{0:T(1024)(128)(4,1)} %bitcast.185), calls=%async_computation.7 | async-start | bytes 1638400
  208.8 1.0 copy-start.5
where the time goes:
time: 223 us; the launch traced here: 221 us
  other arithmetic  135 us (61%)
  local copies, waits for them, and re-layouts  66.7 us (30%)
  starting transfers between devices  11 us (5%)
  loops' own time  5.73 us (3%)
    sub x2, other arithmetic, laplace(): padded[..., 1:-1, 2:] + padded[..., 1:-1, :-2] + padded[..., 2:, 1:-1]  46.9 us
    concatenate x1, local copies, waits for them, and re-layouts, padded_2(): x = jnp.concatenate([before, x, after], axis=dim)  18.3 us
    sub x256, other arithmetic, behind_diff(): lax.slice_in_dim(field, 1, length, axis=axis)  14.7 us
    slice x1, local copies, waits for them, and re-layouts, vertical(): lower = jnp.concatenate([field[1:], field[-1:]], axis=0)  14.1 us
    sub x1, other arithmetic, per_device(): north = mixed[1] - coriolis * ocean_state[0]  13.7 us
    div x64, other arithmetic, subcycle(): (mass * vel_y + sub_step * (force_y + wind_y + drag_coef * ocean_y - turn...  12.8 us
    mul x64, other arithmetic, subcycle(): stress_yy = 0.5 * (sigma_one - sigma_two)  12.7 us
    unnamed x58, local copies, waits for them, and re-layouts  11.5 us
  transfers between devices with their start and end apart: 4, of which 1 were waited for; matrix products, arithmetic and copies ran while one was open for 33% of the time, Pallas kernels for 0%

commit v1 on v0

v1 whole, which is shorter than its diff:
```python
import functools

import jax
import jax.numpy as jnp
from jax import lax
from jax.experimental import pallas as pl
from jax.experimental.pallas import tpu as pltpu
from jax.sharding import PartitionSpec as P

MESH = pl.DeviceIdType.MESH
LANES = 128
SUB = 8
SLAB = 32
SUBCYCLES = 64
THIRD = 2.0 / 3.0


def copies(refs, direction, field, group, peers):
    sbuf, rbuf, ssem, rsem = refs
    return pltpu.make_async_remote_copy(
        src_ref=sbuf.at[direction, field, group],
        dst_ref=rbuf.at[direction, field, group],
        send_sem=ssem.at[direction, field, group],
        recv_sem=rsem.at[direction, field, group],
        device_id=peers[direction],
        device_id_type=MESH,
    )


def edge_copies(refs, field, way, peers):
    esend, erecv, essem, ersem = refs
    return pltpu.make_async_remote_copy(
        src_ref=esend.at[field],
        dst_ref=erecv.at[way, field],
        send_sem=essem.at[way, field],
        recv_sem=ersem.at[way, field],
        device_id=peers[way],
        device_id_type=MESH,
    )


def kernel(
    n_tile,
    n_grp,
    ocean,
    beta,
    prev,
    ice,
    strength,
    mass,
    fraction,
    wind,
    count,
    listed,
    ocean_out,
    ice_out,
    stress_out,
    qb,
    betav,
    prevv,
    iceb,
    state,
    const,
    sbuf,
    rbuf,
    esend,
    erecv,
    qsem,
    bsem,
    isem,
    ssem,
    rsem,
    essem,
    ersem,
):
    fields, blocks, levels = ocean.shape[0], ocean.shape[3] // LANES, ocean.shape[1]
    groups = levels // SUB
    tile = lax.axis_index("tile")
    grp = lax.axis_index("grp")
    above = lax.rem(tile + 1, n_tile)
    below = lax.rem(tile + n_tile - 1, n_tile)
    other = lax.rem(grp + 1, n_grp)
    peers = [{"grp": grp, "tile": above}, {"grp": grp, "tile": below}]
    edge_peers = [
        {"grp": other, "tile": tile},
        {"grp": other, "tile": above},
        {"grp": other, "tile": below},
    ]
    row_refs = (sbuf, rbuf, ssem, rsem)
    edge_refs = (esend, erecv, essem, ersem)
    flat = qb.reshape(fields, blocks + 1, levels * SLAB, LANES)
    ice_view = iceb.reshape(12, blocks, 16, LANES)

    def columns(c):
        return pl.ds(pl.multiple_of(c * LANES, LANES), LANES)

    def load(field, c):
        return pltpu.make_async_copy(
            ocean.at[field, :, :, columns(c)], qb.at[field, c, :, 8:24, :], qsem.at[field, c]
        )

    def ice_loads(c):
        span = columns(c)
        pairs = [
            (ice.at[:, :, span], ice_view.at[0:5, c]),
            (strength.at[:, span], ice_view.at[5, c]),
            (mass.at[:, span], ice_view.at[6, c]),
            (fraction.at[:, span], ice_view.at[7, c]),
            (wind.at[:, :, span], ice_view.at[8:10, c]),
            (ocean.at[0:2, 0, :, span], ice_view.at[10:12, c]),
        ]
        return [pltpu.make_async_copy(s, d, isem.at[n, c]) for n, (s, d) in enumerate(pairs)]

    for field in range(fields):
        pl.loop(0, blocks)(lambda c, field=field: load(field, c).start())

    @pl.loop(0, blocks)
    def _(c):
        for copy in ice_loads(c):
            copy.start()

    beta_copy = pltpu.make_async_copy(beta, betav, bsem.at[0])
    prev_copy = pltpu.make_async_copy(prev, prevv, bsem.at[1])
    beta_copy.start()
    prev_copy.start()

    barrier = pltpu.get_barrier_semaphore()
    for peer in peers + edge_peers:
        pl.semaphore_signal(barrier, inc=1, device_id=peer, device_id_type=MESH)
    pl.semaphore_wait(barrier, 5)

    lane8 = lax.broadcasted_iota(jnp.int32, (SUB, LANES), 1)
    lane16 = lax.broadcasted_iota(jnp.int32, (2 * SUB, LANES), 1)
    for field in range(fields):
        pl.loop(0, blocks)(lambda c, field=field: load(field, c).wait())
        packed = jnp.zeros((2 * SUB, LANES), jnp.float32)
        for level in range(levels):
            ends = jnp.where(
                lane16 < 2, qb[field, 0, level, 8:24, :], qb[field, blocks - 1, level, 8:24, :]
            )
            ends = pltpu.roll(ends, 4 * level + 2, 1)
            packed = jnp.where(lane16 // 4 == level, ends, packed)
        esend[field] = packed
        for way in range(3):
            edge_copies(edge_refs, field, way, edge_peers).start()
        for group in range(groups):

            @pl.loop(0, blocks)
            def _(c):
                first = SLAB * SUB * group + 8
                for row in range(2):
                    sbuf[0, field, group, row, c] = flat[
                        field, c, pl.ds(first + 14 + row, SUB, stride=SLAB), :
                    ]
                    sbuf[1, field, group, row, c] = flat[
                        field, c, pl.ds(first + row, SUB, stride=SLAB), :
                    ]

            for direction in range(2):
                copies(row_refs, direction, field, group, peers).start()

    @pl.loop(0, blocks)
    def _(c):
        for copy in ice_loads(c):
            copy.wait()

    beta_copy.wait()
    prev_copy.wait()

    def ice_row(n, row):
        return jnp.stack(
            [iceb[n, pl.ds(LANES * half + row, SUB, stride=16), :] for half in range(2)]
        )

    for row in range(16):
        sxx, syy = ice_row(2, row), ice_row(3, row)
        state[0, row] = ice_row(0, row)
        state[1, row] = ice_row(1, row)
        state[2, row] = sxx + syy
        state[3, row] = 2.0 * (sxx - syy)
        state[4, row] = 4.0 * ice_row(4, row)
        m = ice_row(6, row)
        inverse = 1.0 / (m + 0.3)
        const[0, row] = (0.5 * THIRD) * ice_row(5, row)
        const[1, row] = m * inverse
        const[2, row] = 0.075 * inverse
        const[3, row] = 0.3 * inverse * (ice_row(8, row) + ice_row(10, row))
        const[4, row] = 0.3 * inverse * (ice_row(9, row) + ice_row(11, row))

    lane = lax.broadcasted_iota(jnp.int32, (2, SUB, LANES), 2)
    is_last = lane == LANES - 1
    is_first = lane == 0

    def ahead_x(q):
        return jnp.where(is_last, 0.0, pltpu.roll(q, LANES - 1, 2) - q)

    def behind_x(q):
        return q - jnp.where(is_first, 0.0, pltpu.roll(q, 1, 2))

    @pl.loop(0, SUBCYCLES)
    def _(step):
        u, v = state[0, 0], state[1, 0]
        before_xy = before_yy = None
        for row in range(16):
            du_dx, dv_dx = ahead_x(u), ahead_x(v)
            if row < 15:
                u_next, v_next = state[0, row + 1], state[1, row + 1]
                du_dy, dv_dy = u_next - u, v_next - v
                div, ten, shr = du_dx + dv_dy, du_dx - dv_dy, du_dy + dv_dx
            else:
                u_next = v_next = None
                div, ten, shr = du_dx, du_dx, dv_dx
            twice = div + div
            root = lax.rsqrt(twice * twice + ten * ten + shr * shr + 1.0)
            pressure = const[0, row]
            scaled = pressure * root
            one = THIRD * state[2, row] + (scaled * twice - pressure)
            two = THIRD * state[3, row] + scaled * ten
            xy = THIRD * state[4, row] + scaled * shr
            state[2, row] = one
            state[3, row] = two
            state[4, row] = xy
            one = one + one
            xx, yy = one + two, one - two
            force_x, force_y = behind_x(xx), behind_x(xy)
            if row:
                force_x, force_y = force_x + (xy - before_xy), force_y + (yy - before_yy)
            else:
                force_x, force_y = force_x + xy, force_y + yy
            before_xy, before_yy = xy, yy
            keep, push = const[1, row], const[2, row]
            state[0, row] = keep * (u + 0.09 * v) + (const[3, row] + push * force_x)
            state[1, row] = keep * (v - 0.09 * u) + (const[4, row] + push * force_y)
            u, v = u_next, v_next

    number = lax.broadcasted_iota(jnp.int32, (2, SUB, LANES), 0) * SUB + lax.broadcasted_iota(
        jnp.int32, (2, SUB, LANES), 1
    )
    covered = jnp.zeros((2, SUB, LANES), jnp.int32)
    for slot in range(blocks):
        block = jnp.where(slot < count[0], listed[0, slot], -1)
        covered = jnp.where(number == block, 1, covered)
    covered = covered > 0
    for row in range(16):
        u, v = state[0, row], state[1, row]
        one, two, xy = state[2, row], state[3, row], state[4, row]
        part = ice_row(7, row)
        results = {
            0: u,
            1: v,
            2: 0.5 * one + 0.25 * two,
            3: 0.5 * one - 0.25 * two,
            4: 0.25 * xy,
            8: part * (u - ice_row(10, row)) + (1.0 - part) * ice_row(8, row),
            9: part * (v - ice_row(11, row)) + (1.0 - part) * ice_row(9, row),
        }
        for n, result in results.items():
            result = jnp.where(covered, result, ice_row(n, row))
            for half in range(2):
                iceb[n, pl.ds(LANES * half + row, SUB, stride=16), :] = result[half]
    for c in range(blocks):
        span = slice(c * LANES, (c + 1) * LANES)
        for n in range(5):
            ice_out[n, :, span] = ice_view[n, c]
        for n in range(2):
            stress_out[n, :, span] = ice_view[8 + n, c]

    has_below = tile > 0
    has_above = tile < n_tile - 1
    place = (tile * 16).astype(jnp.float32) + 0.5
    place = place + lax.broadcasted_iota(jnp.int32, (16, LANES), 0).astype(jnp.float32)
    coriolis = 0.2 * (2.0 * place / (16.0 * n_tile) - 1.0)

    def masked(flag, x):
        return jnp.where(flag, x, jnp.zeros_like(x))

    @pl.loop(0, fields * groups)
    def _(chunk):
        field = lax.div(chunk, groups)
        group = lax.rem(chunk, groups)

        @pl.when(group == 0)
        def _():
            for way in range(3):
                edge_copies(edge_refs, field, way, edge_peers).wait_recv()

        for direction in range(2):
            copies(row_refs, direction, field, group, peers).wait_recv()

        @pl.loop(0, blocks)
        def _(c):
            first = pl.multiple_of(SLAB * SUB * group, SUB)
            for row in range(2):
                flat[field, c, pl.ds(first + 6 + row, SUB, stride=SLAB), :] = masked(
                    has_below, rbuf[0, field, group, row, c]
                )
                flat[field, c, pl.ds(first + 24 + row, SUB, stride=SLAB), :] = masked(
                    has_above, rbuf[1, field, group, row, c]
                )

        for inner in range(SUB):
            level = group * SUB + inner
            shift = lax.rem(2 * LANES - 2 - 4 * level, LANES)
            qb[field, blocks, level, 8:24, :] = pltpu.roll(erecv[0, field], shift, 1)
            qb[field, blocks, level, 0:8, :] = masked(
                has_below, pltpu.roll(erecv[1, field, 8:16], shift, 1)
            )
            qb[field, blocks, level, 24:32, :] = masked(
                has_above, pltpu.roll(erecv[2, field, 0:8], shift, 1)
            )

        turn = jnp.where(field == 0, 1.0, jnp.where(field == 1, -1.0, 0.0)) * coriolis
        partner = jnp.where(field == 0, 1, 0)

        @pl.loop(0, SUB)
        def _(inner):
            level = group * SUB + inner
            upper = jnp.maximum(level - 1, 0)
            lower = jnp.minimum(level + 1, levels - 1)

            def column(c):
                center = qb[field, c, level, 8:24, :]
                near = qb[field, c, level, 7:23, :] + qb[field, c, level, 9:25, :]
                cross = near - 4.0 * center
                return (
                    center,
                    cross,
                    pltpu.roll(center, 2, 1),
                    pltpu.roll(center, LANES - 2, 1),
                    pltpu.roll(cross, 1, 1),
                    pltpu.roll(cross, LANES - 1, 1),
                )

            wrap = column(blocks)
            west, here = wrap, column(0)
            for c in range(blocks):
                east = column(c + 1) if c < blocks - 1 else wrap
                span = slice(c * LANES, (c + 1) * LANES)
                center, cross = here[0], here[1]
                far = qb[field, c, level, 6:22, :] + qb[field, c, level, 10:26, :]
                far = far + jnp.where(lane16 < 2, west[2], here[2])
                far = far + jnp.where(lane16 >= LANES - 2, east[3], here[3])
                near = jnp.where(lane16 < 1, west[4], here[4]) + jnp.where(
                    lane16 >= LANES - 1, east[5], here[5]
                )
                near = near - 4.0 * cross
                smooth = (near + near) + (far - 12.0 * center)
                both = qb[field, c, upper, 8:24, :] + qb[field, c, lower, 8:24, :]
                mixed = (0.6 * center + 0.2 * both) - betav[:, span] * smooth
                ocean_out[field, level, :, span] = mixed + turn * qb[partner, c, level, 8:24, :]
                west, here = here, east

        @pl.when((group == 0) & (field < 2))
        def _():
            for c in range(blocks):
                span = slice(c * LANES, (c + 1) * LANES)
                ocean_out[field, 0, :, span] = ocean_out[field, 0, :, span] + prevv[
                    jnp.minimum(field, 1), :, span
                ]

    @pl.loop(0, fields)
    def _(field):
        for way in range(3):
            edge_copies(edge_refs, field, way, edge_peers).wait_send()

        @pl.loop(0, groups)
        def _(group):
            for direction in range(2):
                copies(row_refs, direction, field, group, peers).wait_send()


def per_device(
    ocean_state,
    biharmonic,
    prev_stress,
    ice_state,
    strength,
    ice_mass,
    ice_fraction,
    wind_stress,
    ice_count,
    ice_list,
):
    fields, levels, rows, cols = ocean_state.shape
    blocks, groups = cols // LANES, levels // SUB
    f32 = jnp.float32
    dma = pltpu.SemaphoreType.DMA
    body = functools.partial(kernel, lax.axis_size("tile"), lax.axis_size("grp"))
    out_spec = pl.BlockSpec(memory_space=pltpu.VMEM)
    return pl.pallas_call(
        body,
        name="coupled",
        out_shape=OUT(ocean_state, ice_state, wind_stress),
        in_specs=[pl.BlockSpec(memory_space=pl.ANY)] * 8
        + [pl.BlockSpec(memory_space=pltpu.SMEM)] * 2,
        out_specs=[out_spec] * 3,
        scratch_shapes=[
            pltpu.VMEM((fields, blocks + 1, levels, SLAB, LANES), f32),
            pltpu.VMEM((rows, cols), f32),
            pltpu.VMEM((2, rows, cols), f32),
            pltpu.VMEM((12, blocks * rows, LANES), f32),
            pltpu.VMEM((5, rows, 2, SUB, LANES), f32),
            pltpu.VMEM((5, rows, 2, SUB, LANES), f32),
            pltpu.VMEM((2, fields, groups, 2, blocks, SUB, LANES), f32),
            pltpu.VMEM((2, fields, groups, 2, blocks, SUB, LANES), f32),
            pltpu.VMEM((fields, rows, LANES), f32),
            pltpu.VMEM((3, fields, rows, LANES), f32),
            dma((fields, blocks)),
            dma((2,)),
            dma((6, blocks)),
            dma((2, fields, groups)),
            dma((2, fields, groups)),
            dma((3, fields)),
            dma((3, fields)),
        ],
        compiler_params=pltpu.CompilerParams(
            collective_id=0, has_side_effects=True, vmem_limit_bytes=VLIM
        ),
    )(
        ocean_state,
        biharmonic,
        prev_stress,
        ice_state,
        strength,
        ice_mass,
        ice_fraction,
        wind_stress,
        ice_count,
        ice_list,
    )


VLIM = 58 << 20


def OUT(*arrays):
    return [jax.ShapeDtypeStruct(a.shape, a.dtype) for a in arrays]


def solution(mesh):
    wide = P(None, "tile", "grp")
    flat = P("tile", "grp")
    deep = P(None, None, "tile", "grp")
    return jax.shard_map(
        per_device,
        mesh=mesh,
        in_specs=(
            deep,
            flat,
            wide,
            wide,
            flat,
            flat,
            flat,
            wide,
            P(("grp", "tile")),
            P(("grp", "tile"), None),
        ),
        out_specs=(deep, wide, wide),
        check_vma=False,
    )
```

time: 223 us -> 70.7 us (0.32)
  the two profiles are of different devices: /device:TPU:96 before, /device:TPU:0 now
where the time goes in v1:
time: 70.7 us; the launch traced here: 70.5 us
  Pallas kernels  58.8 us (83%)
  local copies, waits for them, and re-layouts  10.4 us (15%)
  between operations  1.31 us (2%)
    pallas_call x1, Pallas kernels, per_device(): pl.pallas_call(body, name='coupled', out_shape=OUT(ocean_state, ice_state...  58.8 us
    unnamed x7, local copies, waits for them, and re-layouts  10.4 us

profile of v1, /device:TPU:0, one launch (start us, length us, event | category | flops | bytes accessed | tf_op | source)
XLA Modules:
  0.0 70.5 jit_solution(11983614469558401882)
XLA Ops:
  1.3 58.8 %coupled.1 = (f32[3,24,16,2048]{3,2,1,0:T(8,128)}, f32[5,16,2048]{2,1,0:T(8,128)}, f32[2,16,2048]{2,1,0:T(8,128)}) custom-call(f32[3,24,16,2048]{3,2,1,0:T(8,128)} %ocean.1, f32[16,2048]{1,0:T(8,128)} %beta.1, f32[2,16,2048]{2,1,0:T(8,128)} %prev.1, f32[5,16,2048]{2,1,0:T(8,128)} %ice.1, f32[16,2048]{1,0:T(8,128)} %strength.1, f32[16,2048]{1,0:T(8,128)} %mass.1, ...), custom_call_target="tpu_custom_call" | custom-call | tf_op jit(solution)/shard_map/coupled/pallas_call | solution.py:390
  60.1 0.0 copy-start
  60.1 0.0 copy-start.1
  60.1 8.9 %copy.17 = f32[3,24,16,2048]{3,2,1,0:T(8,128)} copy(f32[3,24,16,2048]{3,2,1,0:T(8,128)} %get-tuple-element.6) | data formatting | bytes 18874368
  69.0 0.0 copy-done
  69.0 0.8 %copy.18 = f32[5,16,2048]{2,1,0:T(8,128)} copy(f32[5,16,2048]{2,1,0:T(8,128)S(1)} %copy-done) | data formatting | bytes 1310720
  69.8 0.0 copy-done.1
  69.8 0.7 copy.19
Async XLA Ops:
  60.1 8.9 %copy-start = (f32[5,16,2048]{2,1,0:T(8,128)S(1)}, f32[5,16,2048]{2,1,0:T(8,128)}, u32[]{:S(2)}) copy-start(f32[5,16,2048]{2,1,0:T(8,128)} %get-tuple-element.7) | copy-start | bytes 1966084
  60.1 9.7 %copy-start.1 = (f32[2,16,2048]{2,1,0:T(8,128)S(1)}, f32[2,16,2048]{2,1,0:T(8,128)}, u32[]{:S(2)}) copy-start(f32[2,16,2048]{2,1,0:T(8,128)} %get-tuple-element.8) | copy-start | bytes 786436

commit v2 on v1

--- a/solution.py
+++ b/solution.py
@@ -127,7 +127,6 @@
     barrier = pltpu.get_barrier_semaphore()
     for peer in peers + edge_peers:
         pl.semaphore_signal(barrier, inc=1, device_id=peer, device_id_type=MESH)
-    pl.semaphore_wait(barrier, 5)
 
     lane8 = lax.broadcasted_iota(jnp.int32, (SUB, LANES), 1)
     lane16 = lax.broadcasted_iota(jnp.int32, (2 * SUB, LANES), 1)
@@ -141,13 +140,11 @@
             ends = pltpu.roll(ends, 4 * level + 2, 1)
             packed = jnp.where(lane16 // 4 == level, ends, packed)
         esend[field] = packed
-        for way in range(3):
-            edge_copies(edge_refs, field, way, edge_peers).start()
         for group in range(groups):
-
-            @pl.loop(0, blocks)
+            first = SLAB * SUB * group + 8
+
+            @pl.loop(0, blocks, unroll=True)
             def _(c):
-                first = SLAB * SUB * group + 8
                 for row in range(2):
                     sbuf[0, field, group, row, c] = flat[
                         field, c, pl.ds(first + 14 + row, SUB, stride=SLAB), :
@@ -156,6 +153,11 @@
                         field, c, pl.ds(first + row, SUB, stride=SLAB), :
                     ]
 
+    pl.semaphore_wait(barrier, 5)
+    for field in range(fields):
+        for way in range(3):
+            edge_copies(edge_refs, field, way, edge_peers).start()
+        for group in range(groups):
             for direction in range(2):
                 copies(row_refs, direction, field, group, peers).start()
 
@@ -197,41 +199,42 @@
     def behind_x(q):
         return q - jnp.where(is_first, 0.0, pltpu.roll(q, 1, 2))
 
-    @pl.loop(0, SUBCYCLES)
-    def _(step):
-        u, v = state[0, 0], state[1, 0]
-        before_xy = before_yy = None
+    def subcycle():
         for row in range(16):
+            u, v = state[0, row], state[1, row]
             du_dx, dv_dx = ahead_x(u), ahead_x(v)
             if row < 15:
-                u_next, v_next = state[0, row + 1], state[1, row + 1]
-                du_dy, dv_dy = u_next - u, v_next - v
+                du_dy, dv_dy = state[0, row + 1] - u, state[1, row + 1] - v
                 div, ten, shr = du_dx + dv_dy, du_dx - dv_dy, du_dy + dv_dx
             else:
-                u_next = v_next = None
                 div, ten, shr = du_dx, du_dx, dv_dx
             twice = div + div
             root = lax.rsqrt(twice * twice + ten * ten + shr * shr + 1.0)
             pressure = const[0, row]
             scaled = pressure * root
-            one = THIRD * state[2, row] + (scaled * twice - pressure)
-            two = THIRD * state[3, row] + scaled * ten
-            xy = THIRD * state[4, row] + scaled * shr
-            state[2, row] = one
-            state[3, row] = two
-            state[4, row] = xy
+            state[2, row] = THIRD * state[2, row] + (scaled * twice - pressure)
+            state[3, row] = THIRD * state[3, row] + scaled * ten
+            state[4, row] = THIRD * state[4, row] + scaled * shr
+        before_yy = None
+        for row in range(16):
+            one, two, xy = state[2, row], state[3, row], state[4, row]
             one = one + one
             xx, yy = one + two, one - two
             force_x, force_y = behind_x(xx), behind_x(xy)
             if row:
-                force_x, force_y = force_x + (xy - before_xy), force_y + (yy - before_yy)
+                force_x, force_y = force_x + (xy - state[4, row - 1]), force_y + (yy - before_yy)
             else:
                 force_x, force_y = force_x + xy, force_y + yy
-            before_xy, before_yy = xy, yy
+            before_yy = yy
             keep, push = const[1, row], const[2, row]
+            u, v = state[0, row], state[1, row]
             state[0, row] = keep * (u + 0.09 * v) + (const[3, row] + push * force_x)
             state[1, row] = keep * (v - 0.09 * u) + (const[4, row] + push * force_y)
-            u, v = u_next, v_next
+
+    @pl.loop(0, SUBCYCLES, step=2)
+    def _(step):
+        subcycle()
+        subcycle()
 
     number = lax.broadcasted_iota(jnp.int32, (2, SUB, LANES), 0) * SUB + lax.broadcasted_iota(
         jnp.int32, (2, SUB, LANES), 1
@@ -287,7 +290,7 @@
         for direction in range(2):
             copies(row_refs, direction, field, group, peers).wait_recv()
 
-        @pl.loop(0, blocks)
+        @pl.loop(0, blocks, unroll=True)
         def _(c):
             first = pl.multiple_of(SLAB * SUB * group, SUB)
             for row in range(2):
@@ -312,8 +315,7 @@
         turn = jnp.where(field == 0, 1.0, jnp.where(field == 1, -1.0, 0.0)) * coriolis
         partner = jnp.where(field == 0, 1, 0)
 
-        @pl.loop(0, SUB)
-        def _(inner):
+        for inner in range(SUB):
             level = group * SUB + inner
             upper = jnp.maximum(level - 1, 0)
             lower = jnp.minimum(level + 1, levels - 1)
@@ -390,8 +392,8 @@
     return pl.pallas_call(
         body,
         name="coupled",
-        out_shape=OUT(ocean_state, ice_state, wind_stress),
-        in_specs=[pl.BlockSpec(memory_space=pl.ANY)] * 8
+        out_shape=[pltpu.VMEM(a.shape, a.dtype) for a in (ocean_state, ice_state, wind_stress)],
+        in_specs=[pl.BlockSpec(memory_space=pltpu.HBM)] * 8
         + [pl.BlockSpec(memory_space=pltpu.SMEM)] * 2,
         out_specs=[out_spec] * 3,
         scratch_shapes=[
@@ -414,7 +416,7 @@
             dma((3, fields)),
         ],
         compiler_params=pltpu.CompilerParams(
-            collective_id=0, has_side_effects=True, vmem_limit_bytes=VLIM
+            collective_id=0, has_side_effects=True, vmem_limit_bytes=44 << 20
         ),
     )(
         ocean_state,
@@ -428,13 +430,6 @@
         ice_count,
         ice_list,
     )
-
-
-VLIM = 58 << 20
-
-
-def OUT(*arrays):
-    return [jax.ShapeDtypeStruct(a.shape, a.dtype) for a in arrays]
 
 
 def solution(mesh):

time: 70.7 us -> 51.6 us (0.73)
  Pallas kernels: 58.8 us -> 44.2 us
  local copies, waits for them, and re-layouts: 10.4 us -> 5.93 us
    pallas_call x1, Pallas kernels: 58.8 us -> 44.2 us  [per_device(): pl.pallas_call(body, name='coupled', out_shape=[pltpu.VMEM(a.shape, a.dty...]
    unnamed x7 -> x5, local copies, waits for them, and re-layouts: 10.4 us -> 5.93 us
where the time goes in v2:
time: 51.6 us; the launch traced here: 51.5 us
  Pallas kernels  44.2 us (86%)
  local copies, waits for them, and re-layouts  5.93 us (11%)
  between operations  1.3 us (3%)
    pallas_call x1, Pallas kernels, per_device(): pl.pallas_call(body, name='coupled', out_shape=[pltpu.VMEM(a.shape, a.dty...  44.2 us
    unnamed x5, local copies, waits for them, and re-layouts  5.93 us

profile of v2, /device:TPU:0, one launch (start us, length us, event | category | flops | bytes accessed | tf_op | source)
XLA Modules:
  0.0 51.5 jit_solution(11205355481339123295)
XLA Ops:
  1.3 0.0 copy-start
  1.3 0.6 %copy-done = s32[1,16]{1,0:T(1,128)S(1)} copy-done((s32[1,16]{1,0:T(1,128)S(1)}, s32[1,16]{1,0:T(1,128)}, u32[]{:S(2)}) %copy-start) | copy-done | bytes 88
  1.9 44.2 %coupled.1 = (f32[3,24,16,2048]{3,2,1,0:T(8,128)S(1)}, f32[5,16,2048]{2,1,0:T(8,128)S(1)}, f32[2,16,2048]{2,1,0:T(8,128)S(1)}) custom-call(f32[3,24,16,2048]{3,2,1,0:T(8,128)} %ocean.1, f32[16,2048]{1,0:T(8,128)} %beta.1, f32[2,16,2048]{2,1,0:T(8,128)} %prev.1, f32[5,16,2048]{2,1,0:T(8,128)} %ice.1, f32[16,2048]{1,0:T(8,128)} %strength.1, f32[16,2048]{1,0:T(8,128)} %mass.1, ...), custom_call_target="tpu_custom_call" | custom-call | tf_op jit(solution)/shard_map/coupled/pallas_call | solution.py:392
  46.2 3.7 %copy.16 = f32[3,24,16,2048]{3,2,1,0:T(8,128)} copy(f32[3,24,16,2048]{3,2,1,0:T(8,128)S(1)} %get-tuple-element.3) | data formatting | bytes 18874368
  49.9 0.7 %copy.18 = f32[2,16,2048]{2,1,0:T(8,128)} copy(f32[2,16,2048]{2,1,0:T(8,128)S(1)} %get-tuple-element.5) | data formatting | bytes 524288
  50.6 0.8 %copy.17 = f32[5,16,2048]{2,1,0:T(8,128)} copy(f32[5,16,2048]{2,1,0:T(8,128)S(1)} %get-tuple-element.4) | data formatting | bytes 1310720
Async XLA Ops:
  1.3 0.7 %copy-start = (s32[1,16]{1,0:T(1,128)S(1)}, s32[1,16]{1,0:T(1,128)}, u32[]{:S(2)}) copy-start(s32[1,16]{1,0:T(1,128)} %listed.1) | copy-start | bytes 196

commit v3 on v2

--- a/solution.py
+++ b/solution.py
@@ -12,6 +12,8 @@
 SUB = 8
 SLAB = 32
 SUBCYCLES = 64
+BEFORE_PACK = 4
+BEFORE_FIRST_ROW = 24
 THIRD = 2.0 / 3.0
 
 
@@ -111,63 +113,57 @@
         ]
         return [pltpu.make_async_copy(s, d, isem.at[n, c]) for n, (s, d) in enumerate(pairs)]
 
-    for field in range(fields):
-        pl.loop(0, blocks)(lambda c, field=field: load(field, c).start())
-
     @pl.loop(0, blocks)
     def _(c):
         for copy in ice_loads(c):
             copy.start()
 
+    for field in range(fields):
+        pl.loop(0, blocks)(lambda c, field=field: load(field, c).start())
+
     beta_copy = pltpu.make_async_copy(beta, betav, bsem.at[0])
     prev_copy = pltpu.make_async_copy(prev, prevv, bsem.at[1])
     beta_copy.start()
     prev_copy.start()
 
+    has_below = tile > 0
+    has_above = tile < n_tile - 1
+    always = tile >= 0
+    sends = [has_above, has_below]
+    receives = [has_below, has_above]
+    edge_sends = [always, has_above, has_below]
+    edge_receives = [always, has_below, has_above]
+
     barrier = pltpu.get_barrier_semaphore()
-    for peer in peers + edge_peers:
-        pl.semaphore_signal(barrier, inc=1, device_id=peer, device_id_type=MESH)
-
-    lane8 = lax.broadcasted_iota(jnp.int32, (SUB, LANES), 1)
+    for peer, exists in zip(peers + edge_peers, sends + edge_sends):
+
+        @pl.when(exists)
+        def _(peer=peer):
+            pl.semaphore_signal(barrier, inc=1, device_id=peer, device_id_type=MESH)
+
     lane16 = lax.broadcasted_iota(jnp.int32, (2 * SUB, LANES), 1)
-    for field in range(fields):
-        pl.loop(0, blocks)(lambda c, field=field: load(field, c).wait())
-        packed = jnp.zeros((2 * SUB, LANES), jnp.float32)
-        for level in range(levels):
-            ends = jnp.where(
-                lane16 < 2, qb[field, 0, level, 8:24, :], qb[field, blocks - 1, level, 8:24, :]
-            )
-            ends = pltpu.roll(ends, 4 * level + 2, 1)
-            packed = jnp.where(lane16 // 4 == level, ends, packed)
-        esend[field] = packed
-        for group in range(groups):
-            first = SLAB * SUB * group + 8
-
-            @pl.loop(0, blocks, unroll=True)
-            def _(c):
-                for row in range(2):
-                    sbuf[0, field, group, row, c] = flat[
-                        field, c, pl.ds(first + 14 + row, SUB, stride=SLAB), :
-                    ]
-                    sbuf[1, field, group, row, c] = flat[
-                        field, c, pl.ds(first + row, SUB, stride=SLAB), :
-                    ]
-
-    pl.semaphore_wait(barrier, 5)
-    for field in range(fields):
-        for way in range(3):
-            edge_copies(edge_refs, field, way, edge_peers).start()
-        for group in range(groups):
-            for direction in range(2):
-                copies(row_refs, direction, field, group, peers).start()
+    def exchange():
+        pl.when(has_below & has_above)(lambda: pl.semaphore_wait(barrier, 5))
+        pl.when(jnp.logical_not(has_below & has_above))(lambda: pl.semaphore_wait(barrier, 3))
+        for field in range(fields):
+            for way in range(3):
+                pl.when(edge_sends[way])(
+                    lambda field=field, way=way: edge_copies(
+                        edge_refs, field, way, edge_peers
+                    ).start()
+                )
+            for group in range(groups):
+                for direction in range(2):
+                    pl.when(sends[direction])(
+                        lambda field=field, group=group, direction=direction: copies(
+                            row_refs, direction, field, group, peers
+                        ).start()
+                    )
 
     @pl.loop(0, blocks)
     def _(c):
         for copy in ice_loads(c):
             copy.wait()
-
-    beta_copy.wait()
-    prev_copy.wait()
 
     def ice_row(n, row):
         return jnp.stack(
@@ -231,17 +227,49 @@
             state[0, row] = keep * (u + 0.09 * v) + (const[3, row] + push * force_x)
             state[1, row] = keep * (v - 0.09 * u) + (const[4, row] + push * force_y)
 
-    @pl.loop(0, SUBCYCLES, step=2)
-    def _(step):
-        subcycle()
-        subcycle()
+    def subcycles(first, last):
+        @pl.loop(first, last, step=2)
+        def _(step):
+            subcycle()
+            subcycle()
+
+    subcycles(0, BEFORE_PACK)
+    for field in range(fields):
+        pl.loop(0, blocks)(lambda c, field=field: load(field, c).wait())
+        packed = jnp.zeros((2 * SUB, LANES), jnp.float32)
+        for level in range(levels):
+            ends = jnp.where(
+                lane16 < 2, qb[field, 0, level, 8:24, :], qb[field, blocks - 1, level, 8:24, :]
+            )
+            ends = pltpu.roll(ends, 4 * level + 2, 1)
+            packed = jnp.where(lane16 // 4 == level, ends, packed)
+        esend[field] = packed
+        for group in range(groups):
+            first = SLAB * SUB * group + 8
+
+            @pl.loop(0, blocks, unroll=True)
+            def _(c):
+                for row in range(2):
+                    sbuf[0, field, group, row, c] = flat[
+                        field, c, pl.ds(first + 14 + row, SUB, stride=SLAB), :
+                    ]
+                    sbuf[1, field, group, row, c] = flat[
+                        field, c, pl.ds(first + row, SUB, stride=SLAB), :
+                    ]
+
+    pl.when(has_below)(exchange)
+    subcycles(BEFORE_PACK, BEFORE_FIRST_ROW)
+    pl.when(jnp.logical_not(has_below))(exchange)
+    subcycles(BEFORE_FIRST_ROW, SUBCYCLES)
+    beta_copy.wait()
+    prev_copy.wait()
 
     number = lax.broadcasted_iota(jnp.int32, (2, SUB, LANES), 0) * SUB + lax.broadcasted_iota(
         jnp.int32, (2, SUB, LANES), 1
     )
     covered = jnp.zeros((2, SUB, LANES), jnp.int32)
     for slot in range(blocks):
-        block = jnp.where(slot < count[0], listed[0, slot], -1)
+        block = jnp.where(slot < count[0], listed[slot], -1)
         covered = jnp.where(number == block, 1, covered)
     covered = covered > 0
     for row in range(16):
@@ -268,14 +296,9 @@
         for n in range(2):
             stress_out[n, :, span] = ice_view[8 + n, c]
 
-    has_below = tile > 0
-    has_above = tile < n_tile - 1
     place = (tile * 16).astype(jnp.float32) + 0.5
     place = place + lax.broadcasted_iota(jnp.int32, (16, LANES), 0).astype(jnp.float32)
     coriolis = 0.2 * (2.0 * place / (16.0 * n_tile) - 1.0)
-
-    def masked(flag, x):
-        return jnp.where(flag, x, jnp.zeros_like(x))
 
     @pl.loop(0, fields * groups)
     def _(chunk):
@@ -285,32 +308,45 @@
         @pl.when(group == 0)
         def _():
             for way in range(3):
-                edge_copies(edge_refs, field, way, edge_peers).wait_recv()
-
-        for direction in range(2):
-            copies(row_refs, direction, field, group, peers).wait_recv()
-
-        @pl.loop(0, blocks, unroll=True)
-        def _(c):
-            first = pl.multiple_of(SLAB * SUB * group, SUB)
-            for row in range(2):
-                flat[field, c, pl.ds(first + 6 + row, SUB, stride=SLAB), :] = masked(
-                    has_below, rbuf[0, field, group, row, c]
+                pl.when(edge_receives[way])(
+                    lambda way=way: edge_copies(edge_refs, field, way, edge_peers).wait_recv()
                 )
-                flat[field, c, pl.ds(first + 24 + row, SUB, stride=SLAB), :] = masked(
-                    has_above, rbuf[1, field, group, row, c]
-                )
+
+        first = pl.multiple_of(SLAB * SUB * group, SUB)
+
+        def shifted(inner, x):
+            return pltpu.roll(x, lax.rem(2 * LANES - 2 - 4 * (group * SUB + inner), LANES), 1)
+
+        for direction, offset, corner in ((0, 6, 0), (1, 24, 24)):
+            part = erecv.at[1, field, 8:16] if direction == 0 else erecv.at[2, field, 0:8]
+
+            @pl.when(receives[direction])
+            def _(direction=direction, offset=offset, corner=corner, part=part):
+                copies(row_refs, direction, field, group, peers).wait_recv()
+
+                @pl.loop(0, blocks, unroll=True)
+                def _(c):
+                    for row in range(2):
+                        flat[field, c, pl.ds(first + offset + row, SUB, stride=SLAB), :] = rbuf[
+                            direction, field, group, row, c
+                        ]
+
+                for inner in range(SUB):
+                    qb[field, blocks, group * SUB + inner, corner : corner + 8, :] = shifted(
+                        inner, part[...]
+                    )
+
+            @pl.when(jnp.logical_not(receives[direction]))
+            def _(offset=offset):
+                @pl.loop(0, blocks + 1)
+                def _(c):
+                    for row in range(2):
+                        flat[field, c, pl.ds(first + offset + row, SUB, stride=SLAB), :] = (
+                            jnp.zeros((SUB, LANES), jnp.float32)
+                        )
 
         for inner in range(SUB):
-            level = group * SUB + inner
-            shift = lax.rem(2 * LANES - 2 - 4 * level, LANES)
-            qb[field, blocks, level, 8:24, :] = pltpu.roll(erecv[0, field], shift, 1)
-            qb[field, blocks, level, 0:8, :] = masked(
-                has_below, pltpu.roll(erecv[1, field, 8:16], shift, 1)
-            )
-            qb[field, blocks, level, 24:32, :] = masked(
-                has_above, pltpu.roll(erecv[2, field, 0:8], shift, 1)
-            )
+            qb[field, blocks, group * SUB + inner, 8:24, :] = shifted(inner, erecv[0, field])
 
         turn = jnp.where(field == 0, 1.0, jnp.where(field == 1, -1.0, 0.0)) * coriolis
         partner = jnp.where(field == 0, 1, 0)
@@ -363,12 +399,31 @@
     @pl.loop(0, fields)
     def _(field):
         for way in range(3):
-            edge_copies(edge_refs, field, way, edge_peers).wait_send()
+            pl.when(edge_sends[way])(
+                lambda way=way: edge_copies(edge_refs, field, way, edge_peers).wait_send()
+            )
 
         @pl.loop(0, groups)
         def _(group):
             for direction in range(2):
-                copies(row_refs, direction, field, group, peers).wait_send()
+                pl.when(sends[direction])(
+                    lambda direction=direction: copies(
+                        row_refs, direction, field, group, peers
+                    ).wait_send()
+                )
+
+
+def store_kernel(ocean, ice, stress, ocean_out, ice_out, stress_out, sem):
+    pieces = [(ice, ice_out), (stress, stress_out)]
+    for field in range(ocean.shape[0]):
+        for half in range(2):
+            span = pl.ds(half * (ocean.shape[1] // 2), ocean.shape[1] // 2)
+            pieces.append((ocean.at[field, span], ocean_out.at[field, span]))
+    started = [pltpu.make_async_copy(a, b, sem.at[n]) for n, (a, b) in enumerate(pieces)]
+    for copy in started:
+        copy.start()
+    for copy in started:
+        copy.wait()
 
 
 def per_device(
@@ -389,7 +444,7 @@
     dma = pltpu.SemaphoreType.DMA
     body = functools.partial(kernel, lax.axis_size("tile"), lax.axis_size("grp"))
     out_spec = pl.BlockSpec(memory_space=pltpu.VMEM)
-    return pl.pallas_call(
+    held = pl.pallas_call(
         body,
         name="coupled",
         out_shape=[pltpu.VMEM(a.shape, a.dtype) for a in (ocean_state, ice_state, wind_stress)],
@@ -428,8 +483,19 @@
         ice_fraction,
         wind_stress,
         ice_count,
-        ice_list,
+        ice_list.reshape(-1),
     )
+    return pl.pallas_call(
+        store_kernel,
+        name="store",
+        out_shape=[
+            jax.ShapeDtypeStruct(a.shape, a.dtype) for a in (ocean_state, ice_state, wind_stress)
+        ],
+        in_specs=[pl.BlockSpec(memory_space=pltpu.VMEM)] * 3,
+        out_specs=[pl.BlockSpec(memory_space=pltpu.HBM)] * 3,
+        scratch_shapes=[dma((2 + 2 * fields,))],
+        compiler_params=pltpu.CompilerParams(vmem_limit_bytes=14 << 20),
+    )(*[pltpu.with_memory_space_constraint(array, pltpu.VMEM) for array in held])
 
 
 def solution(mesh):

time: 51.6 us -> 46.6 us (0.903)
  the two profiles are of different devices: /device:TPU:0 before, /device:TPU:96 now
where the time goes in v3:
time: 46.6 us; the launch traced here: 46.5 us
  Pallas kernels  44.5 us (95%)
  between operations  1.3 us (3%)
  local copies, waits for them, and re-layouts  0.65 us (1%)
    pallas_call x1, Pallas kernels, per_device(): pl.pallas_call(body, name='coupled', out_shape=[pltpu.VMEM(a.shape, a.dty...  40.5 us
    pallas_call x1, Pallas kernels, per_device(): pl.pallas_call(store_kernel, name='store', out_shape=[jax.ShapeDtypeStruc...  4.02 us

profile of v3, /device:TPU:96, one launch (start us, length us, event | category | flops | bytes accessed | tf_op | source)
XLA Modules:
  0.0 46.5 jit_solution(3470013444018566376)
XLA Ops:
  1.3 0.0 copy-start
  1.3 0.6 %copy-done = s32[1,16]{1,0:T(1,128)S(1)} copy-done((s32[1,16]{1,0:T(1,128)S(1)}, s32[1,16]{1,0:T(1,128)}, u32[]{:S(2)}) %copy-start) | copy-done | bytes 88
  1.9 40.5 %coupled.1 = (f32[3,24,16,2048]{3,2,1,0:T(8,128)S(1)}, f32[5,16,2048]{2,1,0:T(8,128)S(1)}, f32[2,16,2048]{2,1,0:T(8,128)S(1)}) custom-call(f32[3,24,16,2048]{3,2,1,0:T(8,128)} %ocean.1, f32[16,2048]{1,0:T(8,128)} %beta.1, f32[2,16,2048]{2,1,0:T(8,128)} %prev.1, f32[5,16,2048]{2,1,0:T(8,128)} %ice.1, f32[16,2048]{1,0:T(8,128)} %strength.1, f32[16,2048]{1,0:T(8,128)} %mass.1, ...), custom_call_target="tpu_custom_call" | custom-call | tf_op jit(solution)/shard_map/coupled/pallas_call | solution.py:447
  42.5 4.0 %store.1 = (f32[3,24,16,2048]{3,2,1,0:T(8,128)}, f32[5,16,2048]{2,1,0:T(8,128)}, f32[2,16,2048]{2,1,0:T(8,128)}) custom-call(f32[3,24,16,2048]{3,2,1,0:T(8,128)S(1)} %get-tuple-element.6.ocean, f32[5,16,2048]{2,1,0:T(8,128)S(1)} %get-tuple-element.7.ice, f32[2,16,2048]{2,1,0:T(8,128)S(1)} %get-tuple-element.8.stress), custom_call_target="tpu_custom_call" | custom-call | tf_op jit(solution)/shard_map/store/pallas_call | solution.py:488
Async XLA Ops:
  1.3 0.7 %copy-start = (s32[1,16]{1,0:T(1,128)S(1)}, s32[1,16]{1,0:T(1,128)}, u32[]{:S(2)}) copy-start(s32[1,16]{1,0:T(1,128)} %param.19) | copy-start | bytes 196

commit v4 on v3

--- a/solution.py
+++ b/solution.py
@@ -12,7 +12,9 @@
 SUB = 8
 SLAB = 32
 SUBCYCLES = 64
-BEFORE_PACK = 4
+BEFORE_PACK = 2
+KERNEL_LIMIT = 35 << 20
+FINISH_LIMIT = 8 << 20
 BEFORE_FIRST_ROW = 24
 THIRD = 2.0 / 3.0
 
@@ -39,6 +41,44 @@
         device_id=peers[way],
         device_id_type=MESH,
     )
+
+
+def ocean_level(q, betav, level, emit):
+    blocks, levels = q.shape[0] - 1, q.shape[1]
+    lane = lax.broadcasted_iota(jnp.int32, (2 * SUB, LANES), 1)
+    upper = jnp.maximum(level - 1, 0)
+    lower = jnp.minimum(level + 1, levels - 1)
+
+    def column(c):
+        center = q[c, level, 8:24, :]
+        near = q[c, level, 7:23, :] + q[c, level, 9:25, :]
+        cross = near - 4.0 * center
+        return (
+            center,
+            cross,
+            pltpu.roll(center, 2, 1),
+            pltpu.roll(center, LANES - 2, 1),
+            pltpu.roll(cross, 1, 1),
+            pltpu.roll(cross, LANES - 1, 1),
+        )
+
+    wrap = column(blocks)
+    west, here = wrap, column(0)
+    for c in range(blocks):
+        east = column(c + 1) if c < blocks - 1 else wrap
+        span = slice(c * LANES, (c + 1) * LANES)
+        center, cross = here[0], here[1]
+        far = q[c, level, 6:22, :] + q[c, level, 10:26, :]
+        far = far + jnp.where(lane < 2, west[2], here[2])
+        far = far + jnp.where(lane >= LANES - 2, east[3], here[3])
+        near = jnp.where(lane < 1, west[4], here[4]) + jnp.where(
+            lane >= LANES - 1, east[5], here[5]
+        )
+        near = near - 4.0 * cross
+        smooth = (near + near) + (far - 12.0 * center)
+        both = q[c, upper, 8:24, :] + q[c, lower, 8:24, :]
+        emit(c, span, (0.6 * center + 0.2 * both) - betav[:, span] * smooth)
+        west, here = here, east
 
 
 def kernel(
@@ -53,12 +93,13 @@
     fraction,
     wind,
     count,
-    listed,
+    listed_hbm,
     ocean_out,
     ice_out,
     stress_out,
     qb,
     betav,
+    listed,
     prevv,
     iceb,
     state,
@@ -123,6 +164,8 @@
 
     beta_copy = pltpu.make_async_copy(beta, betav, bsem.at[0])
     prev_copy = pltpu.make_async_copy(prev, prevv, bsem.at[1])
+    list_copy = pltpu.make_async_copy(listed_hbm, listed, bsem.at[2])
+    list_copy.start()
     beta_copy.start()
     prev_copy.start()
 
@@ -142,23 +185,27 @@
             pl.semaphore_signal(barrier, inc=1, device_id=peer, device_id_type=MESH)
 
     lane16 = lax.broadcasted_iota(jnp.int32, (2 * SUB, LANES), 1)
-    def exchange():
+    def meet():
         pl.when(has_below & has_above)(lambda: pl.semaphore_wait(barrier, 5))
         pl.when(jnp.logical_not(has_below & has_above))(lambda: pl.semaphore_wait(barrier, 3))
-        for field in range(fields):
-            for way in range(3):
-                pl.when(edge_sends[way])(
-                    lambda field=field, way=way: edge_copies(
-                        edge_refs, field, way, edge_peers
+
+    def send(field):
+        for way in range(3):
+            pl.when(edge_sends[way])(
+                lambda way=way: edge_copies(edge_refs, field, way, edge_peers).start()
+            )
+        for group in range(groups):
+            for direction in range(2):
+                pl.when(sends[direction])(
+                    lambda group=group, direction=direction: copies(
+                        row_refs, direction, field, group, peers
                     ).start()
                 )
-            for group in range(groups):
-                for direction in range(2):
-                    pl.when(sends[direction])(
-                        lambda field=field, group=group, direction=direction: copies(
-                            row_refs, direction, field, group, peers
-                        ).start()
-                    )
+
+    def exchange():
+        meet()
+        for field in range(fields):
+            send(field)
 
     @pl.loop(0, blocks)
     def _(c):
@@ -257,10 +304,16 @@
                         field, c, pl.ds(first + row, SUB, stride=SLAB), :
                     ]
 
-    pl.when(has_below)(exchange)
+        @pl.when(has_below)
+        def _(field=field):
+            if field == 0:
+                meet()
+            send(field)
+
     subcycles(BEFORE_PACK, BEFORE_FIRST_ROW)
     pl.when(jnp.logical_not(has_below))(exchange)
     subcycles(BEFORE_FIRST_ROW, SUBCYCLES)
+    list_copy.wait()
     beta_copy.wait()
     prev_copy.wait()
 
@@ -300,11 +353,7 @@
     place = place + lax.broadcasted_iota(jnp.int32, (16, LANES), 0).astype(jnp.float32)
     coriolis = 0.2 * (2.0 * place / (16.0 * n_tile) - 1.0)
 
-    @pl.loop(0, fields * groups)
-    def _(chunk):
-        field = lax.div(chunk, groups)
-        group = lax.rem(chunk, groups)
-
+    def receive(field, group):
         @pl.when(group == 0)
         def _():
             for way in range(3):
@@ -348,53 +397,29 @@
         for inner in range(SUB):
             qb[field, blocks, group * SUB + inner, 8:24, :] = shifted(inner, erecv[0, field])
 
-        turn = jnp.where(field == 0, 1.0, jnp.where(field == 1, -1.0, 0.0)) * coriolis
-        partner = jnp.where(field == 0, 1, 0)
-
+    @pl.loop(0, 2 * groups)
+    def _(chunk):
+        field = lax.div(chunk, groups)
+        group = lax.rem(chunk, groups)
+        receive(field, group)
+        turn = jnp.where(field == 0, 1.0, -1.0) * coriolis
         for inner in range(SUB):
             level = group * SUB + inner
-            upper = jnp.maximum(level - 1, 0)
-            lower = jnp.minimum(level + 1, levels - 1)
-
-            def column(c):
-                center = qb[field, c, level, 8:24, :]
-                near = qb[field, c, level, 7:23, :] + qb[field, c, level, 9:25, :]
-                cross = near - 4.0 * center
-                return (
-                    center,
-                    cross,
-                    pltpu.roll(center, 2, 1),
-                    pltpu.roll(center, LANES - 2, 1),
-                    pltpu.roll(cross, 1, 1),
-                    pltpu.roll(cross, LANES - 1, 1),
+
+            def emit(c, span, mixed, level=level):
+                ocean_out[field, level, :, span] = (
+                    mixed + turn * qb[1 - field, c, level, 8:24, :]
                 )
 
-            wrap = column(blocks)
-            west, here = wrap, column(0)
-            for c in range(blocks):
-                east = column(c + 1) if c < blocks - 1 else wrap
-                span = slice(c * LANES, (c + 1) * LANES)
-                center, cross = here[0], here[1]
-                far = qb[field, c, level, 6:22, :] + qb[field, c, level, 10:26, :]
-                far = far + jnp.where(lane16 < 2, west[2], here[2])
-                far = far + jnp.where(lane16 >= LANES - 2, east[3], here[3])
-                near = jnp.where(lane16 < 1, west[4], here[4]) + jnp.where(
-                    lane16 >= LANES - 1, east[5], here[5]
-                )
-                near = near - 4.0 * cross
-                smooth = (near + near) + (far - 12.0 * center)
-                both = qb[field, c, upper, 8:24, :] + qb[field, c, lower, 8:24, :]
-                mixed = (0.6 * center + 0.2 * both) - betav[:, span] * smooth
-                ocean_out[field, level, :, span] = mixed + turn * qb[partner, c, level, 8:24, :]
-                west, here = here, east
-
-        @pl.when((group == 0) & (field < 2))
+            ocean_level(qb.at[field], betav, level, emit)
+
+        @pl.when(group == 0)
         def _():
             for c in range(blocks):
                 span = slice(c * LANES, (c + 1) * LANES)
-                ocean_out[field, 0, :, span] = ocean_out[field, 0, :, span] + prevv[
-                    jnp.minimum(field, 1), :, span
-                ]
+                ocean_out[field, 0, :, span] = ocean_out[field, 0, :, span] + prevv[field, :, span]
+
+    pl.loop(0, groups)(lambda group: receive(2, group))
 
     @pl.loop(0, fields)
     def _(field):
@@ -413,17 +438,38 @@
                 )
 
 
-def store_kernel(ocean, ice, stress, ocean_out, ice_out, stress_out, sem):
-    pieces = [(ice, ice_out), (stress, stress_out)]
+def finish_kernel(
+    ocean, ice, stress, qb, betav, ocean_out, ice_out, stress_out, stage, sem, stage_sem
+):
+    levels = ocean.shape[1]
+    pieces = []
     for field in range(ocean.shape[0]):
         for half in range(2):
-            span = pl.ds(half * (ocean.shape[1] // 2), ocean.shape[1] // 2)
+            span = pl.ds(half * (levels // 2), levels // 2)
             pieces.append((ocean.at[field, span], ocean_out.at[field, span]))
+    pieces += [(ice, ice_out), (stress, stress_out)]
     started = [pltpu.make_async_copy(a, b, sem.at[n]) for n, (a, b) in enumerate(pieces)]
     for copy in started:
         copy.start()
+
+    def stored(group):
+        span = pl.ds(group * SUB, SUB)
+        return pltpu.make_async_copy(stage.at[span], ocean_out.at[2, span], stage_sem.at[group])
+
+    @pl.loop(0, levels // SUB)
+    def _(group):
+        for inner in range(SUB):
+            level = group * SUB + inner
+
+            def emit(c, span, mixed, level=level):
+                stage[level, :, span] = mixed
+
+            ocean_level(qb.at[2], betav, level, emit)
+        stored(group).start()
+
     for copy in started:
         copy.wait()
+    pl.loop(0, levels // SUB)(lambda group: stored(group).wait())
 
 
 def per_device(
@@ -447,13 +493,18 @@
     held = pl.pallas_call(
         body,
         name="coupled",
-        out_shape=[pltpu.VMEM(a.shape, a.dtype) for a in (ocean_state, ice_state, wind_stress)],
-        in_specs=[pl.BlockSpec(memory_space=pltpu.HBM)] * 8
-        + [pl.BlockSpec(memory_space=pltpu.SMEM)] * 2,
-        out_specs=[out_spec] * 3,
-        scratch_shapes=[
+        out_shape=[
+            pltpu.VMEM((2, levels, rows, cols), f32),
+            pltpu.VMEM(ice_state.shape, f32),
+            pltpu.VMEM(wind_stress.shape, f32),
             pltpu.VMEM((fields, blocks + 1, levels, SLAB, LANES), f32),
             pltpu.VMEM((rows, cols), f32),
+        ],
+        in_specs=[pl.BlockSpec(memory_space=pltpu.HBM)] * 8
+        + [pl.BlockSpec(memory_space=pltpu.SMEM), pl.BlockSpec(memory_space=pltpu.HBM)],
+        out_specs=[out_spec] * 5,
+        scratch_shapes=[
+            pltpu.SMEM((blocks,), jnp.int32),
             pltpu.VMEM((2, rows, cols), f32),
             pltpu.VMEM((12, blocks * rows, LANES), f32),
             pltpu.VMEM((5, rows, 2, SUB, LANES), f32),
@@ -463,7 +514,7 @@
             pltpu.VMEM((fields, rows, LANES), f32),
             pltpu.VMEM((3, fields, rows, LANES), f32),
             dma((fields, blocks)),
-            dma((2,)),
+            dma((3,)),
             dma((6, blocks)),
             dma((2, fields, groups)),
             dma((2, fields, groups)),
@@ -471,7 +522,7 @@
             dma((3, fields)),
         ],
         compiler_params=pltpu.CompilerParams(
-            collective_id=0, has_side_effects=True, vmem_limit_bytes=44 << 20
+            collective_id=0, has_side_effects=True, vmem_limit_bytes=KERNEL_LIMIT
         ),
     )(
         ocean_state,
@@ -486,15 +537,15 @@
         ice_list.reshape(-1),
     )
     return pl.pallas_call(
-        store_kernel,
-        name="store",
+        finish_kernel,
+        name="finish",
         out_shape=[
             jax.ShapeDtypeStruct(a.shape, a.dtype) for a in (ocean_state, ice_state, wind_stress)
         ],
-        in_specs=[pl.BlockSpec(memory_space=pltpu.VMEM)] * 3,
+        in_specs=[out_spec] * 5,
         out_specs=[pl.BlockSpec(memory_space=pltpu.HBM)] * 3,
-        scratch_shapes=[dma((2 + 2 * fields,))],
-        compiler_params=pltpu.CompilerParams(vmem_limit_bytes=14 << 20),
+        scratch_shapes=[pltpu.VMEM((levels, rows, cols), f32), dma((6,)), dma((groups,))],
+        compiler_params=pltpu.CompilerParams(vmem_limit_bytes=FINISH_LIMIT),
     )(*[pltpu.with_memory_space_constraint(array, pltpu.VMEM) for array in held])
 
 

time: 46.6 us -> 43.7 us (0.938)
  Pallas kernels: 44.5 us -> 42.2 us
  local copies, waits for them, and re-layouts: 0.65 us -> 0 us
    pallas_call x2, Pallas kernels: 44.5 us -> 42.2 us  [the longest x1 37.5 us: per_device(): pl.pallas_call(body, name='coupled', out_shape=[pltpu.VMEM((2, levels, ro...]
    unnamed x2 -> x0, local copies, waits for them, and re-layouts: 0.65 us -> none
where the time goes in v4:
time: 43.7 us; the launch traced here: 43.5 us
  Pallas kernels  42.2 us (97%)
  between operations  1.29 us (3%)
    pallas_call x1, Pallas kernels, per_device(): pl.pallas_call(body, name='coupled', out_shape=[pltpu.VMEM((2, levels, ro...  37.5 us
    pallas_call x1, Pallas kernels, per_device(): pl.pallas_call(finish_kernel, name='finish', out_shape=[jax.ShapeDtypeStr...  4.73 us

profile of v4, /device:TPU:96, one launch (start us, length us, event | category | flops | bytes accessed | tf_op | source)
XLA Modules:
  0.0 43.5 jit_solution(16384151115792627037)
XLA Ops:
  1.3 37.5 %coupled.1 = (f32[2,24,16,2048]{3,2,1,0:T(8,128)S(1)}, f32[5,16,2048]{2,1,0:T(8,128)S(1)}, f32[2,16,2048]{2,1,0:T(8,128)S(1)}, f32[3,17,24,32,128]{4,3,2,1,0:T(8,128)S(1)}, f32[16,2048]{1,0:T(8,128)S(1)}) custom-call(f32[3,24,16,2048]{3,2,1,0:T(8,128)} %ocean.1, f32[16,2048]{1,0:T(8,128)} %beta.1, f32[2,16,2048]{2,1,0:T(8,128)} %prev.1, f32[5,16,2048]{2,1,0:T(8,128)} %ice.1, ...), custom_call_target="tpu_custom_call" | custom-call | tf_op jit(solution)/shard_map/coupled/pallas_call | solution.py:493
  38.8 4.7 %finish.1 = (f32[3,24,16,2048]{3,2,1,0:T(8,128)}, f32[5,16,2048]{2,1,0:T(8,128)}, f32[2,16,2048]{2,1,0:T(8,128)}) custom-call(f32[2,24,16,2048]{3,2,1,0:T(8,128)S(1)} %get-tuple-element.8.ocean, f32[5,16,2048]{2,1,0:T(8,128)S(1)} %get-tuple-element.9.ice, f32[2,16,2048]{2,1,0:T(8,128)S(1)} %get-tuple-element.10.stress, ...), custom_call_target="tpu_custom_call" | custom-call | tf_op jit(solution)/shard_map/finish/pallas_call | solution.py:539

commit v5 on v4

--- a/solution.py
+++ b/solution.py
@@ -19,13 +19,13 @@
 THIRD = 2.0 / 3.0
 
 
-def copies(refs, direction, field, group, peers):
+def copies(refs, direction, field, peers):
     sbuf, rbuf, ssem, rsem = refs
     return pltpu.make_async_remote_copy(
-        src_ref=sbuf.at[direction, field, group],
-        dst_ref=rbuf.at[direction, field, group],
-        send_sem=ssem.at[direction, field, group],
-        recv_sem=rsem.at[direction, field, group],
+        src_ref=sbuf.at[direction, field],
+        dst_ref=rbuf.at[direction, field],
+        send_sem=ssem.at[direction, field],
+        recv_sem=rsem.at[direction, field],
         device_id=peers[direction],
         device_id_type=MESH,
     )
@@ -194,13 +194,10 @@
             pl.when(edge_sends[way])(
                 lambda way=way: edge_copies(edge_refs, field, way, edge_peers).start()
             )
-        for group in range(groups):
-            for direction in range(2):
-                pl.when(sends[direction])(
-                    lambda group=group, direction=direction: copies(
-                        row_refs, direction, field, group, peers
-                    ).start()
-                )
+        for direction in range(2):
+            pl.when(sends[direction])(
+                lambda direction=direction: copies(row_refs, direction, field, peers).start()
+            )
 
     def exchange():
         meet()
@@ -371,7 +368,9 @@
 
             @pl.when(receives[direction])
             def _(direction=direction, offset=offset, corner=corner, part=part):
-                copies(row_refs, direction, field, group, peers).wait_recv()
+                pl.when(group == 0)(
+                    lambda: copies(row_refs, direction, field, peers).wait_recv()
+                )
 
                 @pl.loop(0, blocks, unroll=True)
                 def _(c):
@@ -428,14 +427,10 @@
                 lambda way=way: edge_copies(edge_refs, field, way, edge_peers).wait_send()
             )
 
-        @pl.loop(0, groups)
-        def _(group):
-            for direction in range(2):
-                pl.when(sends[direction])(
-                    lambda direction=direction: copies(
-                        row_refs, direction, field, group, peers
-                    ).wait_send()
-                )
+        for direction in range(2):
+            pl.when(sends[direction])(
+                lambda direction=direction: copies(row_refs, direction, field, peers).wait_send()
+            )
 
 
 def finish_kernel(
@@ -516,8 +511,8 @@
             dma((fields, blocks)),
             dma((3,)),
             dma((6, blocks)),
-            dma((2, fields, groups)),
-            dma((2, fields, groups)),
+            dma((2, fields)),
+            dma((2, fields)),
             dma((3, fields)),
             dma((3, fields)),
         ],

time: 43.7 us -> 43.5 us (level)
  no operation moved by 1% of the time
where the time goes in v5:
time: 43.5 us; the launch traced here: 43.3 us
  Pallas kernels  42 us (97%)
  between operations  1.29 us (3%)
    pallas_call x1, Pallas kernels, per_device(): pl.pallas_call(body, name='coupled', out_shape=[pltpu.VMEM((2, levels, ro...  37.3 us
    pallas_call x1, Pallas kernels, per_device(): pl.pallas_call(finish_kernel, name='finish', out_shape=[jax.ShapeDtypeStr...  4.73 us

profile of v5, /device:TPU:96, one launch (start us, length us, event | category | flops | bytes accessed | tf_op | source)
XLA Modules:
  0.0 43.3 jit_solution(9485237077392508774)
XLA Ops:
  1.3 37.3 %coupled.1 = (f32[2,24,16,2048]{3,2,1,0:T(8,128)S(1)}, f32[5,16,2048]{2,1,0:T(8,128)S(1)}, f32[2,16,2048]{2,1,0:T(8,128)S(1)}, f32[3,17,24,32,128]{4,3,2,1,0:T(8,128)S(1)}, f32[16,2048]{1,0:T(8,128)S(1)}) custom-call(f32[3,24,16,2048]{3,2,1,0:T(8,128)} %ocean.1, f32[16,2048]{1,0:T(8,128)} %beta.1, f32[2,16,2048]{2,1,0:T(8,128)} %prev.1, f32[5,16,2048]{2,1,0:T(8,128)} %ice.1, ...), custom_call_target="tpu_custom_call" | custom-call | tf_op jit(solution)/shard_map/coupled/pallas_call | solution.py:488
  38.6 4.7 %finish.1 = (f32[3,24,16,2048]{3,2,1,0:T(8,128)}, f32[5,16,2048]{2,1,0:T(8,128)}, f32[2,16,2048]{2,1,0:T(8,128)}) custom-call(f32[2,24,16,2048]{3,2,1,0:T(8,128)S(1)} %get-tuple-element.8.ocean, f32[5,16,2048]{2,1,0:T(8,128)S(1)} %get-tuple-element.9.ice, f32[2,16,2048]{2,1,0:T(8,128)S(1)} %get-tuple-element.10.stress, ...), custom_call_target="tpu_custom_call" | custom-call | tf_op jit(solution)/shard_map/finish/pallas_call | solution.py:534
